TPU v7x, 256 devices: a whole 4x4x8 slice. The times are simulated.
256 devices in a mesh: role: 2 (over core), dp: 32 (over x, z), mp: 4 (over y).
Axes of the slice: x: 4, y: 4, z: 8, core: 2. Of those that a mesh axis runs over, the one named last changes fastest.
Arguments:
- noise: bfloat16 [4096, 3072], P('dp', 'mp'), may hold values from -6 to 6
- gen_gain: float32 [3072], replicated, may hold values from 0.25 to 1.75
- gen_weight: bfloat16 [3072, 3072], P('dp', 'mp'), may hold values from -0.109375 to 0.109375
- routes: int32 [1024, 1], replicated, may hold values from 0 to 31; in each aligned block of 32 rows (0 to 31, 32 to 63, ...) at most 2 rows name the same one
- critic_noise: bfloat16 [8192, 3072], P('dp', 'mp'), may hold values from -6 to 6
- critic_steps: int32 [2048], P('dp'), may hold values from 20 to 979
- crit_mod: float32 [2, 2, 3072], P('role'), may hold values from -3 to 3
- crit_first: bfloat16 [2, 3072, 3072], P('role', 'dp', 'mp'), may hold values from -0.109375 to 0.109375
- crit_second: bfloat16 [2, 3072, 3072], P('role', 'dp', 'mp'), may hold values from -0.109375 to 0.109375
Outputs:
- noise_grad: float32 [4096, 4, 2, 384], P('dp', 'mp', 'role')
- grad_first: float32 [2, 3072, 3072], P('role', 'dp', 'mp')
- grad_second: float32 [2, 3072, 3072], P('role', 'dp', 'mp')
Inputs may be any that keep to these rules, and one draw needn't show every extreme that they name: `routes`: within the 32 rows of one index of dp, no value appears more than 2 times, and in every draw some value appears exactly 2 times in some such block.
All inputs are finite; a program needn't handle non-finite values.
Results may differ from a plain program's by a relative error of at most 0.01.
Values may be sent and summed in bfloat16 or wider, within the bound.
A program may use at most 128 MiB of HBM per device.

v0:
```python
import jax
import jax.numpy as jnp
from jax import lax
from jax.sharding import Mesh
from jax.sharding import PartitionSpec as P

D = 3072
TOK_DEV = 128
BT = 4
DP = ("dp_0", "dp_1")
epsilon = 1e-06
levels = 1000.0


def copy_for_each(shard, axis):
    length = lax.axis_size(axis)
    return lax.all_to_all(
        jnp.broadcast_to(shard[None], (length, *shard.shape)), axis, 0, 0, tiled=True
    )


def joined_along(pieces, dim):
    pieces = jnp.moveaxis(pieces, 0, dim)
    shape = pieces.shape
    return pieces.reshape(*shape[:dim], shape[dim] * shape[dim + 1], *shape[dim + 2 :])


def collect(shard, axis, dim):
    pieces = copy_for_each(shard, axis)
    return joined_along(pieces, dim)


def summed_rows(shard, axes, dim):
    for axis in axes:
        shard = lax.psum_scatter(shard, axis, scatter_dimension=dim, tiled=True)
    return shard


def cut_along(shard, dim, length):
    before, after = (shard.shape[:dim], shard.shape[dim + 1 :])
    return jnp.moveaxis(shard.reshape(*before, length, -1, *after), dim, 0)


def summed_on_arrival(shard, axis, dim):
    length = lax.axis_size(axis)
    pieces = lax.all_to_all(cut_along(shard, dim, length), axis, 0, 0, tiled=True)
    return jnp.sum(pieces.astype(jnp.float32), axis=0)


def of_everyone(shard, axis):
    return copy_for_each(shard, axis).sum(axis=0)


def from_partner(block, axis, apart):
    count = lax.axis_size(axis)
    route = []
    for low in range(count):
        high = low | 1 << apart
        if high != low and high < count:
            route += [(low, high), (high, low)]
    return lax.ppermute(block, axis, route)


def norm_act(field, scale):
    root = lax.rsqrt(jnp.mean(field * field, axis=-1, keepdims=True) + epsilon)
    normed = field * root
    shaped = normed * scale
    return (jax.nn.silu(shaped).astype(jnp.bfloat16), normed, shaped, root)


def slope(shaped):
    sigma = jax.nn.sigmoid(shaped)
    return sigma * (1.0 + shaped * (1.0 - sigma))


def widen(field):
    return collect(field, "mp", 1)


def layer_rows(weight):
    return lax.all_gather(weight, DP, axis=0, tiled=True)


def weight_sum(left, right):
    term = lax.dot_general(
        left, right, (((0,), (0,)), ((), ())), preferred_element_type=jnp.float32
    )
    return summed_rows(term.astype(jnp.bfloat16), DP, 0).astype(jnp.float32)


def row_back(delta, weight, normed, shaped, root, scale):
    width = weight.shape[1]
    offset = lax.axis_index("mp") * width
    partial_rows = lax.dot_general(
        delta, weight, (((1,), (1,)), ((), ())), preferred_element_type=jnp.float32
    )
    owned = summed_on_arrival(partial_rows.astype(jnp.bfloat16), "mp", 1)
    normed_mine = lax.dynamic_slice_in_dim(normed, offset, width, 1)
    shaped_mine = lax.dynamic_slice_in_dim(shaped, offset, width, 1)
    scale_mine = lax.dynamic_slice_in_dim(jnp.broadcast_to(scale, normed.shape), offset, width, 1)
    grad_norm = owned * slope(shaped_mine) * scale_mine
    inner = of_everyone(jnp.sum(grad_norm * normed_mine, axis=-1), "mp")
    return root * (grad_norm - normed_mine * (inner[:, None] / D))


def shards(
    noise,
    gen_gain,
    gen_weight,
    routes,
    critic_noise,
    critic_steps,
    crit_mod,
    crit_first,
    crit_second,
):
    width = noise.shape[1]
    groups = lax.axis_size(DP)
    me_index = lax.axis_index(DP)
    blocks_here = noise.shape[0] // BT
    most = 2 * blocks_here // groups
    noise_f = noise.astype(jnp.float32)
    gen_scale = gen_gain[None, :]
    gen_act, gen_normed, gen_shaped, gen_root = norm_act(
        widen(noise).astype(jnp.float32), gen_scale
    )
    gen_full = layer_rows(gen_weight)
    generated = (noise_f + jnp.dot(gen_act, gen_full, preferred_element_type=jnp.float32)).astype(
        jnp.bfloat16
    )
    table = routes[:, 0]
    target_index = lax.dynamic_slice_in_dim(table, me_index * blocks_here, blocks_here, 0)
    order = jnp.arange(blocks_here, dtype=jnp.int32)
    earlier = (target_index[:, None] == target_index[None, :]) & (order[None, :] < order[:, None])
    rank = jnp.sum(earlier.astype(jnp.int32), axis=1)
    slot_here = target_index * most + rank
    placing = (jnp.arange(groups * most, dtype=jnp.int32)[:, None] == slot_here[None, :]).astype(
        jnp.bfloat16
    )
    outgoing = jnp.dot(
        placing, generated.reshape(blocks_here, BT * width), preferred_element_type=jnp.float32
    )
    outgoing = outgoing.astype(jnp.bfloat16).reshape(groups, most * BT, width)
    incoming = lax.all_to_all(outgoing, DP, split_axis=0, concat_axis=0, tiled=True)
    clean = incoming.reshape(groups * most * BT, width)
    counts = jnp.sum((table.reshape(groups, blocks_here) == me_index).astype(jnp.int32), axis=1)
    filled = (jnp.arange(most, dtype=jnp.int32)[None, :] < counts[:, None]).astype(jnp.float32)
    valid = jnp.repeat(filled.reshape(groups * most), BT)[:, None]
    level = jnp.repeat(critic_steps.astype(jnp.float32) / levels, BT)[:, None]
    clean_f = clean.astype(jnp.float32)
    crit_noise_f = critic_noise.astype(jnp.float32)
    noisy = ((1.0 - level) * clean_f + level * crit_noise_f).astype(jnp.bfloat16)
    target = crit_noise_f - clean_f
    modulation = crit_mod[0]
    scale_one = 1.0 + level * modulation[0][None, :]
    scale_two = 1.0 + level * modulation[1][None, :]
    first, _, _, _ = norm_act(widen(noisy).astype(jnp.float32), scale_one)
    first_full = layer_rows(crit_first[0])
    first_out = jnp.dot(first, first_full, preferred_element_type=jnp.float32)
    hidden = (noisy.astype(jnp.float32) + first_out).astype(jnp.bfloat16)
    second, normed, shaped, root = norm_act(widen(hidden).astype(jnp.float32), scale_two)
    second_full = layer_rows(crit_second[0])
    pred = (
        hidden.astype(jnp.float32)
        + jnp.dot(second, second_full, preferred_element_type=jnp.float32)
    ).astype(jnp.bfloat16)
    delta = ((pred.astype(jnp.float32) - target) * valid / TOK_DEV).astype(jnp.bfloat16)
    grad_two = weight_sum(second, delta)
    upstream = (
        delta.astype(jnp.float32) + row_back(delta, second_full, normed, shaped, root, scale_two)
    ).astype(jnp.bfloat16)
    grad_one = weight_sum(first, upstream)
    other = from_partner(pred, "role", 0)
    pred_f = pred.astype(jnp.float32)
    other_f = other.astype(jnp.float32)
    difference = jnp.where(lax.axis_index("role") == 1, pred_f - other_f, other_f - pred_f)
    gap = ((1.0 - level) * difference).astype(jnp.bfloat16).reshape(groups, most * BT, width)
    coming_back = lax.all_to_all(gap, DP, split_axis=0, concat_axis=0, tiled=True)
    back_slots = coming_back.reshape(groups * most, BT * width)
    picked = lax.dot_general(
        placing, back_slots, (((0,), (0,)), ((), ())), preferred_element_type=jnp.float32
    )
    returned = picked.astype(jnp.bfloat16).reshape(blocks_here * BT, width)
    noise_grad = returned.astype(jnp.float32) + row_back(
        returned, gen_full, gen_normed, gen_shaped, gen_root, gen_scale
    )
    half_width = width // 2
    my_half = lax.dynamic_slice_in_dim(
        noise_grad, lax.axis_index("role") * half_width, half_width, 1
    )
    return (my_half.reshape(noise_grad.shape[0], 1, 1, half_width), grad_one[None], grad_two[None])


def solution(mesh):
    split = Mesh(
        mesh.devices.reshape(mesh.shape["role"], 4, 8, mesh.shape["mp"]),
        ("role", "dp_0", "dp_1", "mp"),
    )
    in_specs = (
        P(DP, "mp"),
        P(),
        P(DP, "mp"),
        P(),
        P(DP, "mp"),
        P(DP),
        P("role", None, None),
        P("role", DP, "mp"),
        P("role", DP, "mp"),
    )
    out_specs = (P(DP, "mp", "role", None), P("role", DP, "mp"), P("role", DP, "mp"))
    return jax.shard_map(
        shards, mesh=split, in_specs=in_specs, out_specs=out_specs, check_vma=False
    )
```

profile of v0, /device:TPU:2, one launch (start us, length us, event | category | flops | bytes accessed | tf_op | source)
XLA Modules:
  0.0 479.6 jit_solution(8404089671905882432)
XLA Ops:
  10.6 4.5 all-to-all-start
  17.4 9.9 %all-to-all-done = bf16[4,128,768]{2,1,0:T(8,128)(2,1)S(1)} async-done(((bf16[4,128,768]{2,1,0:T(8,128)(2,1)}), bf16[4,128,768]{2,1,0:T(8,128)(2,1)S(1)}, u32[]{:S(2)}, u32[]{:S(2)}) %all-to-all-start) | async-done | bytes 786464 | tf_op jit(solution)/shard_map/all_to_all | solution.py:17
  32.9 62.3 %all-gather.6.cloned.1.call-done = bf16[3072,768]{1,0:T(8,128)(2,1)} async-done(((bf16[96,768]{1,0:T(8,128)(2,1)}), bf16[3072,768]{1,0:T(8,128)(2,1)}) %all-gather.6.cloned.1.call-update) | async-done | bytes 4718608 | tf_op jit(solution)/shard_map/all_gather | solution.py:81
  100.0 7.2 %all-to-all-start.1 = ((bf16[32,8,768]{2,1,0:T(8,128)(2,1)}), bf16[32,8,768]{2,1,0:T(8,128)(2,1)S(1)}, u32[]{:S(2)}, u32[]{:S(2)}) async-start(bf16[32,8,768]{2,1,0:T(8,128)(2,1)} %reshape.127), calls=%async_computation.1 | async-start | bytes 786432 | tf_op jit(solution)/shard_map/all_to_all | solution.py:144
  107.5 11.1 %all-to-all-done.1 = bf16[32,8,768]{2,1,0:T(8,128)(2,1)S(1)} async-done(((bf16[32,8,768]{2,1,0:T(8,128)(2,1)}), bf16[32,8,768]{2,1,0:T(8,128)(2,1)S(1)}, u32[]{:S(2)}, u32[]{:S(2)}) %all-to-all-start.1) | async-done | bytes 393248 | tf_op jit(solution)/shard_map/all_to_all | solution.py:144
  120.1 4.3 all-to-all-start.2
  124.4 14.9 %all-to-all-done.2 = bf16[4,256,768]{2,1,0:T(8,128)(2,1)S(1)} async-done(((bf16[4,256,768]{2,1,0:T(8,128)(2,1)}), bf16[4,256,768]{2,1,0:T(8,128)(2,1)S(1)}, u32[]{:S(2)}, u32[]{:S(2)}) %all-to-all-start.2) | async-done | bytes 1572896 | tf_op jit(solution)/shard_map/all_to_all | solution.py:17
  142.0 36.2 %all-gather.8.cloned.1.call-done = bf16[1,3072,768]{2,1,0:T(8,128)(2,1)} async-done(((bf16[1,96,768]{2,1,0:T(8,128)(2,1)}), bf16[1,3072,768]{2,1,0:T(8,128)(2,1)}) %all-gather.8.cloned.1.call-update) | async-done | bytes 4718608 | tf_op jit(solution)/shard_map/all_gather | solution.py:81
  178.2 5.3 %fusion.20 = bf16[256,768]{1,0:T(8,128)(2,1)S(1)} fusion(bf16[1,3072,768]{2,1,0:T(8,128)(2,1)} %all-gather.8.cloned.1.call-done, bf16[256,768]{1,0:T(8,128)(2,1)S(1)} %fusion.26, f32[256,3072]{1,0:T(8,128)} %bitcast.73, f32[3072]{0:T(1024)S(1)} %bitcast.78, f32[256]{0:T(256)S(1)} %broadcast_in_dim_reshape.4, f32[256]{0:T(256)S(1)} %add_rsqrt_fusion.1), kind=kOutput, calls=%fused_computation.30 | convolution fusion | flops 1215627264 | bytes 8665088 | tf_op jit(solution)/shard_map/dot_general | solution.py:159
  183.6 21.2 %all_to_all.47 = bf16[4,256,768]{2,1,0:T(8,128)(2,1)S(1)} all-to-all(bf16[4,256,768]{2,1,0:T(8,128)(2,1)S(1)} %broadcast_in_dim.27), channel_id=1, replica_groups=mesh['role'=2,'dp_0'=4,'dp_1'=8,'mp'=4] {'mp'}, dimensions={0} | all-to-all | bytes 3145728 | tf_op jit(solution)/shard_map/all_to_all | solution.py:17
  210.2 50.7 %all-gather.10.cloned.1.call-done = bf16[1,3072,768]{2,1,0:T(8,128)(2,1)} async-done(((bf16[1,96,768]{2,1,0:T(8,128)(2,1)}), bf16[1,3072,768]{2,1,0:T(8,128)(2,1)}) %all-gather.10.cloned.1.call-update) | async-done | bytes 4718608 | tf_op jit(solution)/shard_map/all_gather | solution.py:81
  260.9 5.0 %fusion.17 = bf16[256,768]{1,0:T(8,128)(2,1)} fusion(bf16[1,3072,768]{2,1,0:T(8,128)(2,1)} %all-gather.10.cloned.1.call-done, bf16[256,768]{1,0:T(8,128)(2,1)} %copy-done.6, f32[256,3072]{1,0:T(8,128)S(1)} %get-tuple-element.19), kind=kOutput, calls=%fused_computation.29 | convolution fusion | flops 1212481536 | bytes 8650752 | tf_op jit(solution)/shard_map/dot_general | solution.py:165
  274.7 4.3 convolution_convert_fusion
  285.1 4.3 all-to-all-start.7
  289.4 21.4 %all-to-all-done.7 = bf16[4,256,768]{2,1,0:T(8,128)(2,1)S(1)} async-done(((bf16[4,256,768]{2,1,0:T(8,128)(2,1)}), bf16[4,256,768]{2,1,0:T(8,128)(2,1)S(1)}, u32[]{:S(2)}, u32[]{:S(2)}) %all-to-all-start.7) | async-done | bytes 1572896 | tf_op jit(solution)/shard_map/all_to_all | solution.py:46
  314.1 7.6 %all_to_all.48 = f32[4,1,256]{2,1,0:T(1,128)S(1)} all-to-all(f32[4,1,256]{2,1,0:T(1,128)S(1)} %broadcast_in_dim.30), channel_id=1, replica_groups=mesh['role'=2,'dp_0'=4,'dp_1'=8,'mp'=4] {'mp'}, dimensions={0} | all-to-all | bytes 8192 | tf_op jit(solution)/shard_map/all_to_all | solution.py:17
  321.8 6.0 %convolution_convert_fusion.1 = bf16[3072,768]{1,0:T(8,128)(2,1)} fusion(f32[256,768]{1,0:T(8,128)} %get-tuple-element.16, bf16[256,768]{1,0:T(8,128)(2,1)S(1)} %copy-done.5, f32[256,3072]{1,0:T(8,128)} %get-tuple-element.20, s32[]{:T(128)S(6)} %select_n.25, f32[256]{0:T(256)S(1)} %broadcast_multiply_fusion.3, f32[256]{0:T(256)S(1)} %copy-done.18, ...), kind=kOutput, calls=%fused_computation.1 | convolution fusion | flops 1218576384 | bytes 9846788 | tf_op jit(solution)/shard_map/dot_general | solution.py:85
  330.2 9.9 %all-to-all-start.4 = ((bf16[32,8,768]{2,1,0:T(8,128)(2,1)}), bf16[32,8,768]{2,1,0:T(8,128)(2,1)S(1)}, u32[]{:S(2)}, u32[]{:S(2)}) async-start(bf16[32,8,768]{2,1,0:T(8,128)(2,1)} %get-tuple-element.24), calls=%async_computation.4 | async-start | bytes 786432 | tf_op jit(solution)/shard_map/all_to_all | solution.py:178
  340.1 48.6 %reduce-scatter.5.cloned.1.call-done = bf16[768,768]{1,0:T(8,128)(2,1)} async-done(((bf16[3072,768]{1,0:T(8,128)(2,1)}), bf16[768,768]{1,0:T(8,128)(2,1)}) %reduce-scatter.5.cloned.1.call-update) | async-done | bytes 1179664 | tf_op jit(solution)/shard_map/reduce_scatter | solution.py:35
  394.3 4.3 all-to-all-start.5
  399.4 11.5 %all-to-all-done.5 = bf16[4,128,768]{2,1,0:T(8,128)(2,1)S(1)} async-done(((bf16[4,128,768]{2,1,0:T(8,128)(2,1)}), bf16[4,128,768]{2,1,0:T(8,128)(2,1)S(1)}, u32[]{:S(2)}, u32[]{:S(2)}) %all-to-all-start.5) | async-done | bytes 786464 | tf_op jit(solution)/shard_map/all_to_all | solution.py:46
  416.2 5.2 %all-to-all-done.6 = f32[4,1,128]{2,1,0:T(1,128)S(1)} async-done(((f32[4,1,128]{2,1,0:T(1,128)}), f32[4,1,128]{2,1,0:T(1,128)S(1)}, u32[]{:S(2)}, u32[]{:S(2)}) %all-to-all-start.6) | async-done | bytes 2080 | tf_op jit(solution)/shard_map/all_to_all | solution.py:17
  423.3 7.0 %reduce-scatter.11.cloned.1.call-done = bf16[96,768]{1,0:T(8,128)(2,1)} async-done(((bf16[768,768]{1,0:T(8,128)(2,1)}), bf16[96,768]{1,0:T(8,128)(2,1)}) %reduce-scatter.11.cloned.1.call-update) | async-done | bytes 147472 | tf_op jit(solution)/shard_map/reduce_scatter | solution.py:35
  431.9 39.2 %reduce-scatter.7.cloned.1.call-done = bf16[96,768]{1,0:T(8,128)(2,1)} async-done(((bf16[768,768]{1,0:T(8,128)(2,1)}), bf16[96,768]{1,0:T(8,128)(2,1)}) %reduce-scatter.7.cloned.1.call-update) | async-done | bytes 147472 | tf_op jit(solution)/shard_map/reduce_scatter | solution.py:35
  (126 shorter events, 63.5 us)
Async XLA Ops:
  7.2 88.1 %all-gather.6.cloned.1.call-start = ((), (), s32[]{:S(2)}) async-start(), calls=%async_computation.13 | async-start | bytes 4866048 | tf_op jit(solution)/shard_map/all_gather | solution.py:81
  7.9 170.3 %all-gather.8.cloned.1.call-start = ((), (), s32[]{:S(2)}) async-start(), calls=%async_computation.18 | async-start | bytes 4866048 | tf_op jit(solution)/shard_map/all_gather | solution.py:81
  10.6 16.7 %all-to-all-start = ((bf16[4,128,768]{2,1,0:T(8,128)(2,1)}), bf16[4,128,768]{2,1,0:T(8,128)(2,1)S(1)}, u32[]{:S(2)}, u32[]{:S(2)}) async-start(bf16[4,128,768]{2,1,0:T(8,128)(2,1)} %broadcast_in_dim.25), calls=%async_computation | async-start | bytes 1572864 | tf_op jit(solution)/shard_map/all_to_all | solution.py:17
  15.0 245.9 %all-gather.10.cloned.1.call-start = ((), (), s32[]{:S(2)}) async-start(), calls=%async_computation.19 | async-start | bytes 4866048 | tf_op jit(solution)/shard_map/all_gather | solution.py:81
  17.4 81.4 %copy-start.15 = (s32[32]{0:T(128)}, s32[32]{0:T(128)S(1)}, u32[]{:S(2)}) copy-start(s32[32]{0:T(128)S(1)} %multiply_add_fusion.1) | copy-start | bytes 388
  29.5 65.8 %copy-start.7 = (bf16[128,768]{1,0:T(8,128)(2,1)S(1)}, bf16[128,768]{1,0:T(8,128)(2,1)}, u32[]{:S(2)}) copy-start(bf16[128,768]{1,0:T(8,128)(2,1)} %param.9) | copy-start | bytes 589828
  29.9 65.3 %copy-start.19 = (f32[128]{0:T(128)}, f32[128]{0:T(128)S(1)}, u32[]{:S(2)}) copy-start(f32[128]{0:T(128)S(1)} %add_rsqrt_fusion.2) | copy-start | bytes 1540
  32.9 65.7 %copy-start.2 = (f32[128,3072]{1,0:T(8,128)}, f32[128,3072]{1,0:T(8,128)S(1)}, u32[]{:S(2)}) copy-start(f32[128,3072]{1,0:T(8,128)S(1)} %get-tuple-element.21) | copy-start | bytes 4718596
  100.0 18.6 %all-to-all-start.1 = ((bf16[32,8,768]{2,1,0:T(8,128)(2,1)}), bf16[32,8,768]{2,1,0:T(8,128)(2,1)S(1)}, u32[]{:S(2)}, u32[]{:S(2)}) async-start(bf16[32,8,768]{2,1,0:T(8,128)(2,1)} %reshape.127), calls=%async_computation.1 | async-start | bytes 786432 | tf_op jit(solution)/shard_map/all_to_all | solution.py:144
  107.5 98.3 %copy-start.10 = (f32[256]{0:T(256)}, f32[256]{0:T(256)S(1)}, u32[]{:S(2)}) copy-start(f32[256]{0:T(256)S(1)} %broadcast_in_dim_reshape.4) | copy-start | bytes 3076
  120.1 19.2 %all-to-all-start.2 = ((bf16[4,256,768]{2,1,0:T(8,128)(2,1)}), bf16[4,256,768]{2,1,0:T(8,128)(2,1)S(1)}, u32[]{:S(2)}, u32[]{:S(2)}) async-start(bf16[4,256,768]{2,1,0:T(8,128)(2,1)} %broadcast_in_dim.26), calls=%async_computation.2 | async-start | bytes 3145728 | tf_op jit(solution)/shard_map/all_to_all | solution.py:17
  124.4 205.8 %reduce-scatter.9.cloned.1.call-start = ((), (), s32[]{:S(2)}) async-start(), calls=%async_computation.16 | async-start | bytes 5898240 | tf_op jit(solution)/shard_map/reduce_scatter | solution.py:35
  124.4 53.8 %copy-start.12 = (f32[1,1,3072]{2,1,0:T(1,128)}, f32[1,1,3072]{2,1,0:T(1,128)S(1)}, u32[]{:S(2)}) copy-start(f32[1,1,3072]{2,1,0:T(1,128)S(1)} %get-tuple-element.26) | copy-start | bytes 36868
  142.0 41.5 %copy-start.21 = (f32[256]{0:T(256)}, f32[256]{0:T(256)S(1)}, u32[]{:S(2)}) copy-start(f32[256]{0:T(256)S(1)} %add_rsqrt_fusion.1) | copy-start | bytes 3076
  210.2 63.7 %copy-start = (f32[256,3072]{1,0:T(8,128)}, f32[256,3072]{1,0:T(8,128)S(1)}, u32[]{:S(2)}) copy-start(f32[256,3072]{1,0:T(8,128)S(1)} %get-tuple-element.19) | copy-start | bytes 9437188
  265.9 5.7 %collective-permute-start = (bf16[256,768]{1,0:T(8,128)(2,1)}, bf16[256,768]{1,0:T(8,128)(2,1)}, u32[]{:S(2)}, u32[]{:S(2)}) collective-permute-start(bf16[256,768]{1,0:T(8,128)(2,1)} %fusion.17), channel_id=1, source_target_pairs={{0,128},{128,0},{1,129},{129,1},{2,130},{130,2},{3,131},{131,3},{4... | collective-permute-start | bytes 1179656 | tf_op jit(solution)/shard_map/ppermute | solution.py:61
  285.1 25.7 %all-to-all-start.7 = ((bf16[4,256,768]{2,1,0:T(8,128)(2,1)}), bf16[4,256,768]{2,1,0:T(8,128)(2,1)S(1)}, u32[]{:S(2)}, u32[]{:S(2)}) async-start(bf16[4,256,768]{2,1,0:T(8,128)(2,1)} %bitcast.68), calls=%async_computation.7 | async-start | bytes 3145728 | tf_op jit(solution)/shard_map/all_to_all | solution.py:46
  289.4 99.3 %reduce-scatter.5.cloned.1.call-start = ((), (), s32[]{:S(2)}) async-start(), calls=%async_computation.14 | async-start | bytes 5898240 | tf_op jit(solution)/shard_map/reduce_scatter | solution.py:35
  327.8 61.1 %copy-start.16 = (s32[32]{0:T(128)S(1)}, s32[32]{0:T(128)}, u32[]{:S(2)}) copy-start(s32[32]{0:T(128)} %copy-done.15) | copy-start | bytes 388
  327.9 102.4 %reduce-scatter.11.cloned.1.call-start = ((), (), s32[]{:S(2)}) async-start(), calls=%async_computation.17 | async-start | bytes 1327104 | tf_op jit(solution)/shard_map/reduce_scatter | solution.py:35
  330.2 58.5 %all-to-all-start.4 = ((bf16[32,8,768]{2,1,0:T(8,128)(2,1)}), bf16[32,8,768]{2,1,0:T(8,128)(2,1)S(1)}, u32[]{:S(2)}, u32[]{:S(2)}) async-start(bf16[32,8,768]{2,1,0:T(8,128)(2,1)} %get-tuple-element.24), calls=%async_computation.4 | async-start | bytes 786432 | tf_op jit(solution)/shard_map/all_to_all | solution.py:178
  340.0 131.1 %reduce-scatter.7.cloned.1.call-start = ((), (), s32[]{:S(2)}) async-start(), calls=%async_computation.15 | async-start | bytes 1327104 | tf_op jit(solution)/shard_map/reduce_scatter | solution.py:35
  394.3 16.6 %all-to-all-start.5 = ((bf16[4,128,768]{2,1,0:T(8,128)(2,1)}), bf16[4,128,768]{2,1,0:T(8,128)(2,1)S(1)}, u32[]{:S(2)}, u32[]{:S(2)}) async-start(bf16[4,128,768]{2,1,0:T(8,128)(2,1)} %bitcast.70), calls=%async_computation.5 | async-start | bytes 1572864 | tf_op jit(solution)/shard_map/all_to_all | solution.py:46
  412.9 8.4 %all-to-all-start.6 = ((f32[4,1,128]{2,1,0:T(1,128)}), f32[4,1,128]{2,1,0:T(1,128)S(1)}, u32[]{:S(2)}, u32[]{:S(2)}) async-start(f32[4,1,128]{2,1,0:T(1,128)} %broadcast_in_dim.28), calls=%async_computation.6 | async-start | bytes 4096 | tf_op jit(solution)/shard_map/all_to_all | solution.py:17
  (14 other events, 199.7 us)
Sparse Core Ops, SparseCore 0:
  10.5 84.6 all-gather.5
  97.8 80.3 all-gather.7
  180.8 80.0 all-gather.9
  279.1 50.9 reduce-scatter.8
  332.5 56.0 reduce-scatter.4
  391.1 39.1 reduce-scatter.10
  432.8 38.2 reduce-scatter.6
where the time goes:
time: 481 us; the launch traced here: 480 us
  waiting for transfers between devices  322 us (67%)
  starting transfers between devices  37.8 us (8%)
  matrix products  32.2 us (7%)
  blocking collectives  28.8 us (6%)
  other arithmetic  23.3 us (5%)
  local copies, waits for them, and re-layouts  20.8 us (4%)
  between operations  14.5 us (3%)
    all_gather x3, waiting for transfers between devices, layer_rows(): return lax.all_gather(weight, DP, axis=0, tiled=True)  149 us
    reduce_scatter x4, waiting for transfers between devices, summed_rows(): shard = lax.psum_scatter(shard, axis, scatter_dimension=dim, tiled=True)  97 us
    all_to_all x2, waiting for transfers between devices, summed_on_arrival(): lax.all_to_all(cut_along(shard, dim, length), axis, 0, 0, tiled=True)  32.9 us
    all_to_all x3, waiting for transfers between devices, copy_for_each(): lax.all_to_all(jnp.broadcast_to(shard[None], (length, *shard.shape)), axi...  29.9 us
    all_to_all x2, blocking collectives, copy_for_each(): lax.all_to_all(jnp.broadcast_to(shard[None], (length, *shard.shape)), axi...  28.8 us
    all_to_all x3, starting transfers between devices, copy_for_each(): lax.all_to_all(jnp.broadcast_to(shard[None], (length, *shard.shape)), axi...  12 us
    all_to_all x1, waiting for transfers between devices, shards(): lax.all_to_all(outgoing, DP, split_axis=0, concat_axis=0, tiled=True)  11.1 us
    dot_general x2, matrix products, weight_sum(): lax.dot_general(left, right, (((0,), (0,)), ((), ())), preferred_element_...  10.3 us
  transfers between devices with their start and end apart: 15, of which 13 were waited for; matrix products, arithmetic and copies ran while one was open for 13% of the time, Pallas kernels for 0%

commit v1 on v0

--- a/solution.py
+++ b/solution.py
@@ -78,7 +78,9 @@
 
 
 def layer_rows(weight):
-    return lax.all_gather(weight, DP, axis=0, tiled=True)
+    return jnp.concatenate(
+        lax.all_to_all(jnp.stack([weight] * lax.axis_size(DP)), DP, 0, 0), axis=0
+    )
 
 
 def weight_sum(left, right):

time: 481 us -> 671 us (1.40)
  waiting for transfers between devices: 322 us -> 436 us
  starting transfers between devices: 37.8 us -> 69.9 us
  blocking collectives: 28.8 us -> 56 us
  local copies, waits for them, and re-layouts: 20.8 us -> 34 us
    all_to_all x0 -> x3, waiting for transfers between devices: none -> 290 us  [layer_rows(): lax.all_to_all(jnp.stack([weight] * lax.axis_size(DP)), DP, 0, 0)]
    all_gather x3 -> x0, waiting for transfers between devices: 149 us -> none  [layer_rows(): return lax.all_gather(weight, DP, axis=0, tiled=True)]
    all_to_all x0 -> x3, starting transfers between devices: none -> 34.4 us  [layer_rows(): lax.all_to_all(jnp.stack([weight] * lax.axis_size(DP)), DP, 0, 0)]
    all_to_all x2 -> x3, blocking collectives: 28.8 us -> 56 us  [copy_for_each(): lax.all_to_all(jnp.broadcast_to(shard[None], (length, *shard.shape)), axi...]
    all_to_all x3 -> x2, waiting for transfers between devices: 29.9 us -> 5.92 us  [copy_for_each(): lax.all_to_all(jnp.broadcast_to(shard[None], (length, *shard.shape)), axi...]
    reduce_scatter x4, waiting for transfers between devices: 97 us -> 84.2 us  [summed_rows(): shard = lax.psum_scatter(shard, axis, scatter_dimension=dim, tiled=True)]
    all_to_all x1, waiting for transfers between devices: 0.01 us -> 10.6 us  [shards(): lax.all_to_all(gap, DP, split_axis=0, concat_axis=0, tiled=True)]
    another operation x0 -> x3, local copies, waits for them, and re-layouts: none -> 9.06 us  [layer_rows(): jnp.stack([weight] * lax.axis_size(DP))]
  transfers between devices with their start and end apart: 15 -> 14, of which waited for: 13 -> 13; matrix products, arithmetic and copies ran while one was open for 13% -> 9% of each run, Pallas kernels for 0% -> 0%
where the time goes in v1:
time: 671 us; the launch traced here: 670 us
  waiting for transfers between devices  436 us (65%)
  starting transfers between devices  69.9 us (10%)
  blocking collectives  56 us (8%)
  local copies, waits for them, and re-layouts  34 us (5%)
  other arithmetic  29.9 us (4%)
  matrix products  29.9 us (4%)
  between operations  14.3 us (2%)
    all_to_all x3, waiting for transfers between devices, layer_rows(): lax.all_to_all(jnp.stack([weight] * lax.axis_size(DP)), DP, 0, 0)  290 us
    reduce_scatter x4, waiting for transfers between devices, summed_rows(): shard = lax.psum_scatter(shard, axis, scatter_dimension=dim, tiled=True)  84.2 us
    all_to_all x3, blocking collectives, copy_for_each(): lax.all_to_all(jnp.broadcast_to(shard[None], (length, *shard.shape)), axi...  56 us
    all_to_all x3, starting transfers between devices, layer_rows(): lax.all_to_all(jnp.stack([weight] * lax.axis_size(DP)), DP, 0, 0)  34.4 us
    all_to_all x2, waiting for transfers between devices, summed_on_arrival(): lax.all_to_all(cut_along(shard, dim, length), axis, 0, 0, tiled=True)  32.5 us
  transfers between devices with their start and end apart: 14, of which 13 were waited for; matrix products, arithmetic and copies ran while one was open for 9% of the time, Pallas kernels for 0%

profile of v1, /device:TPU:2, one launch (start us, length us, event | category | flops | bytes accessed | tf_op | source)
XLA Modules:
  0.0 670.0 jit_solution(9840461869124121993)
XLA Ops:
  8.1 16.6 %all_to_all.62 = bf16[4,128,768]{2,1,0:T(8,128)(2,1)S(1)} all-to-all(bf16[4,128,768]{2,1,0:T(8,128)(2,1)S(1)} %broadcast_in_dim.25), channel_id=1, replica_groups=mesh['role'=2,'dp_0'=4,'dp_1'=8,'mp'=4] {'mp'}, dimensions={0} | all-to-all | bytes 1572864 | tf_op jit(solution)/shard_map/all_to_all | solution.py:17
  28.3 11.8 %all-to-all-start.1 = ((bf16[32,96,768]{2,1,0:T(8,128)(2,1)}), bf16[32,96,768]{2,1,0:T(8,128)(2,1)}, u32[]{:S(2)}, u32[]{:S(2)}) async-start(bf16[32,96,768]{2,1,0:T(8,128)(2,1)} %stack.6), calls=%async_computation.1 | async-start | bytes 9437184 | tf_op jit(solution)/shard_map/all_to_all | solution.py:82
  43.2 98.5 %all-to-all-done.1 = bf16[32,96,768]{2,1,0:T(8,128)(2,1)} async-done(((bf16[32,96,768]{2,1,0:T(8,128)(2,1)}), bf16[32,96,768]{2,1,0:T(8,128)(2,1)}, u32[]{:S(2)}, u32[]{:S(2)}) %all-to-all-start.1) | async-done | bytes 4718624 | tf_op jit(solution)/shard_map/all_to_all | solution.py:82
  146.4 10.8 %all-to-all-start.2 = ((bf16[32,8,768]{2,1,0:T(8,128)(2,1)}), bf16[32,8,768]{2,1,0:T(8,128)(2,1)S(1)}, u32[]{:S(2)}, u32[]{:S(2)}) async-start(bf16[32,8,768]{2,1,0:T(8,128)(2,1)} %reshape.184), calls=%async_computation.2 | async-start | bytes 786432 | tf_op jit(solution)/shard_map/all_to_all | solution.py:146
  157.4 12.9 %all-to-all-done.2 = bf16[32,8,768]{2,1,0:T(8,128)(2,1)S(1)} async-done(((bf16[32,8,768]{2,1,0:T(8,128)(2,1)}), bf16[32,8,768]{2,1,0:T(8,128)(2,1)S(1)}, u32[]{:S(2)}, u32[]{:S(2)}) %all-to-all-start.2) | async-done | bytes 393248 | tf_op jit(solution)/shard_map/all_to_all | solution.py:146
  171.3 19.9 %all_to_all.63 = bf16[4,256,768]{2,1,0:T(8,128)(2,1)S(1)} all-to-all(bf16[4,256,768]{2,1,0:T(8,128)(2,1)S(1)} %broadcast_in_dim.26), channel_id=1, replica_groups=mesh['role'=2,'dp_0'=4,'dp_1'=8,'mp'=4] {'mp'}, dimensions={0} | all-to-all | bytes 3145728 | tf_op jit(solution)/shard_map/all_to_all | solution.py:17
  194.0 9.4 %all-to-all-start.4 = ((bf16[32,96,768]{2,1,0:T(8,128)(2,1)}), bf16[32,96,768]{2,1,0:T(8,128)(2,1)}, u32[]{:S(2)}, u32[]{:S(2)}) async-start(bf16[32,96,768]{2,1,0:T(8,128)(2,1)} %stack.7), calls=%async_computation.4 | async-start | bytes 9437184 | tf_op jit(solution)/shard_map/all_to_all | solution.py:82
  208.8 97.9 %all-to-all-done.4 = bf16[32,96,768]{2,1,0:T(8,128)(2,1)} async-done(((bf16[32,96,768]{2,1,0:T(8,128)(2,1)}), bf16[32,96,768]{2,1,0:T(8,128)(2,1)}, u32[]{:S(2)}, u32[]{:S(2)}) %all-to-all-start.4) | async-done | bytes 4718624 | tf_op jit(solution)/shard_map/all_to_all | solution.py:82
  310.7 19.5 %all_to_all.64 = bf16[4,256,768]{2,1,0:T(8,128)(2,1)} all-to-all(bf16[4,256,768]{2,1,0:T(8,128)(2,1)S(1)} %broadcast_in_dim.27), channel_id=1, replica_groups=mesh['role'=2,'dp_0'=4,'dp_1'=8,'mp'=4] {'mp'}, dimensions={0} | all-to-all | bytes 3145728 | tf_op jit(solution)/shard_map/all_to_all | solution.py:17
  333.0 13.2 %all-to-all-start.6 = ((bf16[32,96,768]{2,1,0:T(8,128)(2,1)}), bf16[32,96,768]{2,1,0:T(8,128)(2,1)}, u32[]{:S(2)}, u32[]{:S(2)}) async-start(bf16[32,96,768]{2,1,0:T(8,128)(2,1)} %stack.8), calls=%async_computation.6 | async-start | bytes 9437184 | tf_op jit(solution)/shard_map/all_to_all | solution.py:82
  354.9 93.4 %all-to-all-done.6 = bf16[32,96,768]{2,1,0:T(8,128)(2,1)} async-done(((bf16[32,96,768]{2,1,0:T(8,128)(2,1)}), bf16[32,96,768]{2,1,0:T(8,128)(2,1)}, u32[]{:S(2)}, u32[]{:S(2)}) %all-to-all-start.6) | async-done | bytes 4718624 | tf_op jit(solution)/shard_map/all_to_all | solution.py:82
  448.3 4.3 fusion.10
  456.3 5.7 fusion.12
  463.9 4.2 convolution_convert_fusion
  476.8 21.6 %all-to-all-done.10 = bf16[4,256,768]{2,1,0:T(8,128)(2,1)S(1)} async-done(((bf16[4,256,768]{2,1,0:T(8,128)(2,1)}), bf16[4,256,768]{2,1,0:T(8,128)(2,1)S(1)}, u32[]{:S(2)}, u32[]{:S(2)}) %all-to-all-start.10) | async-done | bytes 1572896 | tf_op jit(solution)/shard_map/all_to_all | solution.py:46
  511.9 6.0 convolution_convert_fusion.1
  520.9 10.1 %all-to-all-start.7 = ((bf16[32,8,768]{2,1,0:T(8,128)(2,1)}), bf16[32,8,768]{2,1,0:T(8,128)(2,1)S(1)}, u32[]{:S(2)}, u32[]{:S(2)}) async-start(bf16[32,8,768]{2,1,0:T(8,128)(2,1)} %get-tuple-element.24), calls=%async_computation.7 | async-start | bytes 786432 | tf_op jit(solution)/shard_map/all_to_all | solution.py:180
  533.6 10.6 %all-to-all-done.7 = bf16[32,8,768]{2,1,0:T(8,128)(2,1)S(1)} async-done(((bf16[32,8,768]{2,1,0:T(8,128)(2,1)}), bf16[32,8,768]{2,1,0:T(8,128)(2,1)S(1)}, u32[]{:S(2)}, u32[]{:S(2)}) %all-to-all-start.7) | async-done | bytes 393248 | tf_op jit(solution)/shard_map/all_to_all | solution.py:180
  544.5 35.1 %reduce-scatter.5.cloned.1.call-done = bf16[768,768]{1,0:T(8,128)(2,1)} async-done(((bf16[3072,768]{1,0:T(8,128)(2,1)}), bf16[768,768]{1,0:T(8,128)(2,1)}) %reduce-scatter.5.cloned.1.call-update) | async-done | bytes 1179664 | tf_op jit(solution)/shard_map/reduce_scatter | solution.py:35
  585.1 4.3 all-to-all-start.8
  590.7 10.9 %all-to-all-done.8 = bf16[4,128,768]{2,1,0:T(8,128)(2,1)S(1)} async-done(((bf16[4,128,768]{2,1,0:T(8,128)(2,1)}), bf16[4,128,768]{2,1,0:T(8,128)(2,1)S(1)}, u32[]{:S(2)}, u32[]{:S(2)}) %all-to-all-start.8) | async-done | bytes 786464 | tf_op jit(solution)/shard_map/all_to_all | solution.py:46
  606.9 5.2 all-to-all-done.9
  614.0 7.5 %reduce-scatter.11.cloned.1.call-done = bf16[96,768]{1,0:T(8,128)(2,1)} async-done(((bf16[768,768]{1,0:T(8,128)(2,1)}), bf16[96,768]{1,0:T(8,128)(2,1)}) %reduce-scatter.11.cloned.1.call-update) | async-done | bytes 147472 | tf_op jit(solution)/shard_map/reduce_scatter | solution.py:35
  623.1 38.7 %reduce-scatter.7.cloned.1.call-done = bf16[96,768]{1,0:T(8,128)(2,1)} async-done(((bf16[768,768]{1,0:T(8,128)(2,1)}), bf16[96,768]{1,0:T(8,128)(2,1)}) %reduce-scatter.7.cloned.1.call-update) | async-done | bytes 147472 | tf_op jit(solution)/shard_map/reduce_scatter | solution.py:35
  (149 shorter events, 87.8 us)
Async XLA Ops:
  28.3 113.4 %all-to-all-start.1 = ((bf16[32,96,768]{2,1,0:T(8,128)(2,1)}), bf16[32,96,768]{2,1,0:T(8,128)(2,1)}, u32[]{:S(2)}, u32[]{:S(2)}) async-start(bf16[32,96,768]{2,1,0:T(8,128)(2,1)} %stack.6), calls=%async_computation.1 | async-start | bytes 9437184 | tf_op jit(solution)/shard_map/all_to_all | solution.py:82
  40.1 101.6 %copy-start.7 = (bf16[128,768]{1,0:T(8,128)(2,1)S(1)}, bf16[128,768]{1,0:T(8,128)(2,1)}, u32[]{:S(2)}) copy-start(bf16[128,768]{1,0:T(8,128)(2,1)} %param.9) | copy-start | bytes 589828
  41.9 103.2 %copy-start.23 = (s32[32]{0:T(128)}, s32[32]{0:T(128)S(1)}, u32[]{:S(2)}) copy-start(s32[32]{0:T(128)S(1)} %multiply_add_fusion.1) | copy-start | bytes 388
  42.3 102.7 %copy-start = (bf16[4,128,768]{1,2,0:T(8,128)(2,1)}, bf16[4,128,768]{1,2,0:T(8,128)(2,1)S(1)}, u32[]{:S(2)}) copy-start(bf16[4,128,768]{1,2,0:T(8,128)(2,1)S(1)} %copy.52) | copy-start | bytes 2359300
  42.7 99.0 %copy-start.25 = (f32[128]{0:T(128)}, f32[128]{0:T(128)S(1)}, u32[]{:S(2)}) copy-start(f32[128]{0:T(128)S(1)} %add_rsqrt_fusion.2) | copy-start | bytes 1540
  141.7 28.5 %copy-start.4 = (bf16[256,768]{1,0:T(8,128)(2,1)S(1)}, bf16[256,768]{1,0:T(8,128)(2,1)}, u32[]{:S(2)}) copy-start(bf16[256,768]{1,0:T(8,128)(2,1)} %param.13) | copy-start | bytes 1179652
  146.4 23.9 %all-to-all-start.2 = ((bf16[32,8,768]{2,1,0:T(8,128)(2,1)}), bf16[32,8,768]{2,1,0:T(8,128)(2,1)S(1)}, u32[]{:S(2)}, u32[]{:S(2)}) async-start(bf16[32,8,768]{2,1,0:T(8,128)(2,1)} %reshape.184), calls=%async_computation.2 | async-start | bytes 786432 | tf_op jit(solution)/shard_map/all_to_all | solution.py:146
  157.4 33.8 %copy-start.17 = (f32[256]{0:T(256)}, f32[256]{0:T(256)S(1)}, u32[]{:S(2)}) copy-start(f32[256]{0:T(256)S(1)} %broadcast_subtract_fusion) | copy-start | bytes 3076
  157.4 33.8 %copy-start.11 = (bf16[1,96,768]{2,1,0:T(8,128)(2,1)S(1)}, bf16[1,96,768]{2,1,0:T(8,128)(2,1)}, u32[]{:S(2)}) copy-start(bf16[1,96,768]{2,1,0:T(8,128)(2,1)} %param.16) | copy-start | bytes 442372
  194.0 112.8 %all-to-all-start.4 = ((bf16[32,96,768]{2,1,0:T(8,128)(2,1)}), bf16[32,96,768]{2,1,0:T(8,128)(2,1)}, u32[]{:S(2)}, u32[]{:S(2)}) async-start(bf16[32,96,768]{2,1,0:T(8,128)(2,1)} %stack.7), calls=%async_computation.4 | async-start | bytes 9437184 | tf_op jit(solution)/shard_map/all_to_all | solution.py:82
  310.6 19.7 %copy-start.10 = (bf16[256,768]{1,0:T(8,128)(2,1)}, bf16[256,768]{1,0:T(8,128)(2,1)S(1)}, u32[]{:S(2)}) copy-start(bf16[256,768]{1,0:T(8,128)(2,1)S(1)} %fusion.9) | copy-start | bytes 1179652
  310.6 19.7 %copy-start.12 = (bf16[1,96,768]{2,1,0:T(8,128)(2,1)S(1)}, bf16[1,96,768]{2,1,0:T(8,128)(2,1)}, u32[]{:S(2)}) copy-start(bf16[1,96,768]{2,1,0:T(8,128)(2,1)} %param.17) | copy-start | bytes 442372
  333.0 115.4 %all-to-all-start.6 = ((bf16[32,96,768]{2,1,0:T(8,128)(2,1)}), bf16[32,96,768]{2,1,0:T(8,128)(2,1)}, u32[]{:S(2)}, u32[]{:S(2)}) async-start(bf16[32,96,768]{2,1,0:T(8,128)(2,1)} %stack.8), calls=%async_computation.6 | async-start | bytes 9437184 | tf_op jit(solution)/shard_map/all_to_all | solution.py:82
  346.2 174.7 %reduce-scatter.9.cloned.1.call-start = ((), (), s32[]{:S(2)}) async-start(), calls=%async_computation.18 | async-start | bytes 5898240 | tf_op jit(solution)/shard_map/reduce_scatter | solution.py:35
  452.6 9.4 %collective-permute-start = (bf16[256,768]{1,0:T(8,128)(2,1)S(1)}, bf16[256,768]{1,0:T(8,128)(2,1)S(1)}, u32[]{:S(2)}, u32[]{:S(2)}) collective-permute-start(bf16[256,768]{1,0:T(8,128)(2,1)S(1)} %fusion.10), channel_id=1, source_target_pairs={{0,128},{128,0},{1,129},{129,1},{2,130},{130,2},{3,131},{131,3},{4... | collective-permute-start | bytes 1179656 | tf_op jit(solution)/shard_map/ppermute | solution.py:61
  473.2 25.2 %all-to-all-start.10 = ((bf16[4,256,768]{2,1,0:T(8,128)(2,1)}), bf16[4,256,768]{2,1,0:T(8,128)(2,1)S(1)}, u32[]{:S(2)}, u32[]{:S(2)}) async-start(bf16[4,256,768]{2,1,0:T(8,128)(2,1)} %bitcast.88), calls=%async_computation.10 | async-start | bytes 3145728 | tf_op jit(solution)/shard_map/all_to_all | solution.py:46
  502.1 8.5 %all-to-all-start.11 = ((f32[4,1,256]{2,1,0:T(1,128)}), f32[4,1,256]{2,1,0:T(1,128)S(1)}, u32[]{:S(2)}, u32[]{:S(2)}) async-start(f32[4,1,256]{2,1,0:T(1,128)} %broadcast_in_dim.30), calls=%async_computation.11 | async-start | bytes 8192 | tf_op jit(solution)/shard_map/all_to_all | solution.py:17
  505.4 74.2 %reduce-scatter.5.cloned.1.call-start = ((), (), s32[]{:S(2)}) async-start(), calls=%async_computation.16 | async-start | bytes 5898240 | tf_op jit(solution)/shard_map/reduce_scatter | solution.py:35
  517.9 103.6 %reduce-scatter.11.cloned.1.call-start = ((), (), s32[]{:S(2)}) async-start(), calls=%async_computation.19 | async-start | bytes 1327104 | tf_op jit(solution)/shard_map/reduce_scatter | solution.py:35
  520.9 23.3 %all-to-all-start.7 = ((bf16[32,8,768]{2,1,0:T(8,128)(2,1)}), bf16[32,8,768]{2,1,0:T(8,128)(2,1)S(1)}, u32[]{:S(2)}, u32[]{:S(2)}) async-start(bf16[32,8,768]{2,1,0:T(8,128)(2,1)} %get-tuple-element.24), calls=%async_computation.7 | async-start | bytes 786432 | tf_op jit(solution)/shard_map/all_to_all | solution.py:180
  531.0 130.8 %reduce-scatter.7.cloned.1.call-start = ((), (), s32[]{:S(2)}) async-start(), calls=%async_computation.17 | async-start | bytes 1327104 | tf_op jit(solution)/shard_map/reduce_scatter | solution.py:35
  531.9 47.7 %copy-start.24 = (s32[32]{0:T(128)S(1)}, s32[32]{0:T(128)}, u32[]{:S(2)}) copy-start(s32[32]{0:T(128)} %copy-done.23) | copy-start | bytes 388
  585.1 16.6 %all-to-all-start.8 = ((bf16[4,128,768]{2,1,0:T(8,128)(2,1)}), bf16[4,128,768]{2,1,0:T(8,128)(2,1)S(1)}, u32[]{:S(2)}, u32[]{:S(2)}) async-start(bf16[4,128,768]{2,1,0:T(8,128)(2,1)} %bitcast.85), calls=%async_computation.8 | async-start | bytes 1572864 | tf_op jit(solution)/shard_map/all_to_all | solution.py:46
  603.6 8.4 %all-to-all-start.9 = ((f32[4,1,128]{2,1,0:T(1,128)}), f32[4,1,128]{2,1,0:T(1,128)S(1)}, u32[]{:S(2)}, u32[]{:S(2)}) async-start(f32[4,1,128]{2,1,0:T(1,128)} %broadcast_in_dim.28), calls=%async_computation.9 | async-start | bytes 4096 | tf_op jit(solution)/shard_map/all_to_all | solution.py:17
  (21 other events, 142.1 us)
Sparse Core Ops, SparseCore 0:
  468.2 52.6 reduce-scatter.8
  523.4 56.1 reduce-scatter.4
  582.2 39.2 reduce-scatter.10
  623.9 37.8 reduce-scatter.6
